TPU v7x, 256 devices: a whole 4x4x8 slice. The times are simulated.
256 devices in a mesh: seq: 32 (over z, x), win: 4 (over y), wout: 2 (over core).
Axes of the slice: x: 4, y: 4, z: 8, core: 2. Of those that a mesh axis runs over, the one named last changes fastest.
Arguments:
- qkv_in: bfloat16 [8192, 3, 2048], P('seq', None, ('win', 'wout')), may hold values from -6 to 6
- conv_w: float32 [3, 4, 2048], P(None, None, ('win', 'wout')), may hold values from -3 to 3
- beta_logits: float32 [16, 8192], P(('win', 'wout'), 'seq'), may hold values from -10 to 3
- lengths: int32 [4], replicated, may hold values from 1 to 3968, as said below
- out_gain: float32 [128], replicated, may hold values from 0.1 to 1.9
- w_out: bfloat16 [2048, 2048], P(('win', 'wout')), may hold values from -0.125 to 0.125
- hidden_in: bfloat16 [8192, 2048], P(('seq', 'win', 'wout')), may hold values from -6 to 6
- norm_gain: float32 [2048], replicated, may hold values from 0.1 to 1.9
- w_qkv: bfloat16 [2048, 6144], P('win', 'wout'), may hold values from -0.125 to 0.125
Outputs:
- qkv_next: bfloat16 [8192, 6144], P(('seq', 'win'), 'wout')
- stream_out: bfloat16 [8192, 2048], P(('seq', 'win', 'wout'))
- final_states: float32 [4, 16, 128, 128], P(None, ('win', 'wout'))
- conv_edges: bfloat16 [4, 3, 3, 2048], P(None, None, None, ('win', 'wout'))
Inputs may be any that keep to these rules, and one draw needn't show every extreme that they name: The lengths sum to 8192; the largest is exactly 3968.
All inputs are finite; a program needn't handle non-finite values.
Results may differ from a plain program's by a relative error of at most 0.022.
Values may be sent and summed in bfloat16 or wider, within the bound.
No kernel may reach another device: no remote copies, remote signals or barrier semaphores. Data moves between devices by JAX's collectives and lax.ppermute only.
A program may use at most 64 MiB of HBM per device.

v0:
```python
import jax
import jax.numpy as jnp
from jax import lax
from jax.sharding import PartitionSpec as P

DK = 128
CONV = 4
SPAN = 64
REQS = 4


def from_behind(value, axis, steps):
    count = lax.axis_size(axis)
    leading, last = (max(0, -steps), min(count, count - steps))
    return lax.ppermute(value, axis, [(source, source + steps) for source in range(leading, last)])


def segment_ids(positions, seg_ends):
    counts = jnp.sum((positions[:, None] >= seg_ends[None, :]).astype(jnp.int32), axis=1)
    return jnp.where(positions < 0, -1, counts)


def unit_rows(values):
    return values / jnp.sqrt(jnp.sum(values * values, axis=-1, keepdims=True) + 1e-06)


def outer_product(form, left, right):
    return jnp.einsum(form, left, right, precision=lax.Precision.HIGHEST)


def body(qkv_in, conv_w, beta_logits, lengths, out_gain, w_out, hidden_in, norm_gain, w_qkv):
    row_count = qkv_in.shape[0]
    local_width = qkv_in.shape[2]
    head_count = local_width // DK
    rim_rows = CONV - 1
    first_position = lax.axis_index("seq") * row_count
    seg_ends = jnp.cumsum(lengths)
    preceding_entries = from_behind(qkv_in[row_count - rim_rows :], "seq", 1)
    extended = jnp.concatenate([preceding_entries, qkv_in], axis=0)
    ext_pos = first_position - rim_rows + jnp.arange(row_count + rim_rows, dtype=jnp.int32)
    ext_seg = segment_ids(ext_pos, seg_ends)
    own_seg = ext_seg[rim_rows:]
    pre = jnp.zeros((row_count, 3, local_width), jnp.float32)
    for offset in range(CONV):
        same_request = (ext_seg[offset : offset + row_count] == own_seg).astype(jnp.float32)
        window = extended[offset : offset + row_count].astype(jnp.float32)
        pre = pre + conv_w[:, offset, :][None] * window * same_request[:, None, None]
    activated = jax.nn.silu(pre).astype(jnp.bfloat16)
    span_count = row_count // SPAN

    def blocks(values):
        return values.reshape(span_count, SPAN, head_count, DK).transpose(0, 2, 1, 3)

    query = blocks(
        unit_rows(activated[:, 0].astype(jnp.float32).reshape(row_count, head_count, DK))
    )
    keys_b = blocks(
        unit_rows(activated[:, 1].astype(jnp.float32).reshape(row_count, head_count, DK))
    )
    values_b = blocks(activated[:, 2].astype(jnp.float32).reshape(row_count, head_count, DK))
    beta_coefficient = (
        jax.nn.sigmoid(beta_logits).reshape(head_count, span_count, SPAN).transpose(1, 0, 2)
    )
    seg_blocks = own_seg.reshape(span_count, SPAN)
    before_seg = segment_ids(
        first_position + jnp.arange(span_count, dtype=jnp.int32) * SPAN - 1, seg_ends
    )
    coupled_entries = (seg_blocks == before_seg[:, None]).astype(jnp.float32)
    same = seg_blocks[:, :, None] == seg_blocks[:, None, :]
    row_ids = jnp.arange(SPAN)[:, None]
    col_ids = jnp.arange(SPAN)[None, :]
    strict = (same & (row_ids > col_ids)).astype(jnp.float32)
    causal = (same & (row_ids >= col_ids)).astype(jnp.float32)
    gram = outer_product("nhik,nhjk->nhij", keys_b, keys_b)
    system = (
        jnp.eye(SPAN, dtype=jnp.float32) + beta_coefficient[..., :, None] * gram * strict[:, None]
    )
    targets = jnp.concatenate(
        [
            beta_coefficient[..., None] * values_b,
            (beta_coefficient * coupled_entries[:, None])[..., None] * keys_b,
        ],
        axis=-1,
    )
    solved = lax.linalg.triangular_solve(
        system, targets, left_side=True, lower=True, unit_diagonal=True
    )
    u_local = solved[..., :DK]
    w_link = solved[..., DK:]
    scores = outer_product("nhik,nhjk->nhij", query, keys_b) * causal[:, None]
    out_local = outer_product("nhij,nhjv->nhiv", scores, u_local)
    query_link = coupled_entries[:, None, :, None] * query - outer_product(
        "nhij,nhjk->nhik", scores, w_link
    )
    eye_keys = jnp.eye(DK, dtype=jnp.float32)
    last_link = coupled_entries[:, -1]
    in_last = (seg_blocks == seg_blocks[:, -1:]).astype(jnp.float32)
    trans = last_link[:, None, None, None] * (
        eye_keys - outer_product("nhjk,nhjl->nhkl", keys_b, w_link)
    )
    write = outer_product("nhjk,nhjv->nhkv", keys_b * in_last[:, None, :, None], u_local)

    def fold_span(carried_state, state_pair):
        return (
            (
                outer_product("hkl,hlm->hkm", state_pair[0], carried_state[0]),
                outer_product("eat,eto->eao", state_pair[0], carried_state[1]) + state_pair[1],
            ),
            None,
        )

    identity_maps = (
        jnp.broadcast_to(eye_keys, (head_count, DK, DK)),
        jnp.zeros((head_count, DK, DK), jnp.float32),
    )
    (device_transition, device_update), unused = lax.scan(fold_span, identity_maps, (trans, write))

    def chain_step(hop_index, incoming_state):
        outgoing_state = (
            outer_product("eat,eto->eao", device_transition, incoming_state) + device_update
        )
        return from_behind(outgoing_state, "seq", 1)

    state_in = lax.fori_loop(0, lax.axis_size("seq") - 1, chain_step, jnp.zeros_like(device_update))

    def advance(memory_state, state_pair):
        return (
            outer_product("eat,eto->eao", state_pair[0], memory_state) + state_pair[1],
            memory_state,
        )

    unused_end, entry_states = lax.scan(advance, state_in, (trans, write))
    attended = out_local + outer_product("nhik,nhkv->nhiv", query_link, entry_states)
    corrected_values = u_local - outer_product("nhik,nhkv->nhiv", w_link, entry_states)
    positions = (first_position + jnp.arange(row_count, dtype=jnp.int32)).reshape(span_count, SPAN)
    last_tok = seg_ends - 1
    at_end = (positions[None] == last_tok[:, None, None]).astype(jnp.float32)
    ends_here = jnp.sum(at_end, axis=2)
    request_ids = jnp.arange(REQS, dtype=jnp.int32)
    member = (seg_blocks[None] == request_ids[:, None, None]).astype(jnp.float32) * ends_here[
        ..., None
    ]
    carried = jnp.sum(at_end * coupled_entries[None], axis=2)
    req_states = outer_product("rn,nhkv->rhkv", carried, entry_states)
    req_states = req_states + jnp.einsum(
        "rnj,nhjk,nhjv->rhkv", member, keys_b, corrected_values, precision=lax.Precision.HIGHEST
    )
    owned = (last_tok >= first_position) & (last_tok < first_position + row_count)
    wanted = last_tok[:, None] - rim_rows + 1 + jnp.arange(rim_rows, dtype=jnp.int32)[None, :]
    select = (
        (ext_pos[None, None, :] == wanted[:, :, None])
        & (ext_seg[None, None, :] == request_ids[:, None, None])
        & owned[:, None, None]
    )
    edge_vals = jnp.einsum(
        "rim,mcj->ricj", select.astype(jnp.bfloat16), extended, preferred_element_type=jnp.float32
    )
    totals = (
        lax.psum(req_states.astype(jnp.bfloat16), "seq").astype(jnp.float32),
        lax.psum(edge_vals.astype(jnp.bfloat16), "seq").astype(jnp.float32),
    )
    final_states = totals[0]
    conv_edges = totals[1].astype(jnp.bfloat16)
    heads_rows = attended.transpose(0, 2, 1, 3).reshape(row_count, head_count, DK)
    scale_heads = jnp.sqrt(jnp.mean(heads_rows * heads_rows, axis=-1, keepdims=True) + 1e-05)
    normed_heads = (
        (heads_rows / scale_heads * out_gain).reshape(row_count, local_width).astype(jnp.bfloat16)
    )
    mixed = lax.psum_scatter(
        jnp.dot(normed_heads, w_out, preferred_element_type=jnp.float32).astype(jnp.bfloat16),
        ("win", "wout"),
        scatter_dimension=0,
        tiled=True,
    ).astype(jnp.float32)
    summed = hidden_in.astype(jnp.float32) + mixed
    stream_out = summed.astype(jnp.bfloat16)
    scale_stream = jnp.sqrt(jnp.mean(summed * summed, axis=-1, keepdims=True) + 1e-05)
    normed_stream = (summed / scale_stream * norm_gain).astype(jnp.bfloat16)
    in_block = w_qkv.shape[0]
    all_rows = lax.all_gather(normed_stream, ("win", "wout"), axis=0, tiled=True)
    columns = lax.dynamic_slice_in_dim(all_rows, lax.axis_index("win") * in_block, in_block, 1)
    projected = lax.psum_scatter(
        jnp.dot(columns, w_qkv, preferred_element_type=jnp.float32).astype(jnp.bfloat16),
        "win",
        scatter_dimension=0,
        tiled=True,
    )
    return (projected, stream_out, final_states, conv_edges)


def solution(mesh):
    return jax.shard_map(
        body,
        mesh=mesh,
        in_specs=(
            P("seq", None, ("win", "wout")),
            P(None, None, ("win", "wout")),
            P(("win", "wout"), "seq"),
            P(),
            P(),
            P(("win", "wout"), None),
            P(("seq", "win", "wout"), None),
            P(),
            P("win", "wout"),
        ),
        out_specs=(
            P(("seq", "win"), "wout"),
            P(("seq", "win", "wout"), None),
            P(None, ("win", "wout"), None, None),
            P(None, None, None, ("win", "wout")),
        ),
        check_vma=False,
    )
```

profile of v0, /device:TPU:16, one launch (start us, length us, event | category | flops | bytes accessed | tf_op | source)
XLA Modules:
  0.0 699.0 jit_solution(7639928728784033836)
XLA Ops:
  8.9 3.5 collective-permute-start.1
  45.6 40.7 %custom-call.3 = f32[4,2,1,64,64]{3,4,2,1,0:T(8,128)} custom-call(f32[4,2,1,64,64]{4,3,2,1,0:T(8,128)} %fusion.23), custom_call_target="InvertDiagBlocksLowerTriangular" | custom-call | tf_op jit(solution)/shard_map/triangular_solve | solution.py:85
  98.1 9.9 %while.37 = (s32[]{:T(128)}, f32[2,128,128]{2,1,0:T(8,128)S(1)}, f32[2,128,128]{2,1,0:T(8,128)S(1)}, f32[4,2,128,128]{3,2,1,0:T(8,128)}, f32[4,2,128,128]{3,2,1,0:T(8,128)}, /*index=5*/s32[]{:T(128)}, s32[]{:T(128)}) while((s32[]{:T(128)}, f32[2,128,128]{2,1,0:T(8,128)S(1)}, f32[2,128,128]{2,1,0:T(8,128)S(1)}, ...), condition=%wide.region_6.7_spmd.clone, body=%wide.region_5.6_spmd.clone.sunk | while | flops 100728832 | bytes 1443426 | solution.py:116
  108.1 306.8 %while.35 = (s32[]{:T(128)}, f32[2,128,128]{2,1,0:T(8,128)S(1)}, f32[2,128,128]{2,1,0:T(8,128)S(1)}, f32[2,128,128]{2,1,0:T(8,128)S(1)}, s32[]{:T(128)}) while((s32[]{:T(128)}, f32[2,128,128]{2,1,0:T(8,128)S(1)}, f32[2,128,128]{2,1,0:T(8,128)S(1)}, f32[2,128,128]{2,1,0:T(8,128)S(1)}, s32[]{:T(128)}) %tuple.81), condition=%wide.region_8.9_spmd, body=%wide.region_7.8_spmd.sunk | while | flops 50364416 | bytes 1048677 | solution.py:124
  109.0 3.4 collective-permute-start
  116.2 4.2 collective-permute-start
  124.2 4.2 collective-permute-start
  132.2 4.2 collective-permute-start
  140.1 4.2 collective-permute-start
  148.1 6.0 collective-permute-start
  157.8 6.3 collective-permute-start
  167.9 6.5 collective-permute-start
  174.4 3.9 collective-permute-done
  179.2 6.9 collective-permute-start
  186.1 3.4 collective-permute-done
  190.5 6.1 collective-permute-start
  200.3 5.9 collective-permute-start
  210.0 6.4 collective-permute-start
  220.1 6.4 collective-permute-start
  230.3 6.3 collective-permute-start
  240.4 6.3 collective-permute-start
  250.5 6.3 collective-permute-start
  256.8 3.5 collective-permute-done
  261.3 6.7 collective-permute-start
  268.0 3.7 collective-permute-done
  272.6 6.7 collective-permute-start
  283.0 6.0 collective-permute-start
  292.8 6.4 collective-permute-start
  302.9 6.4 collective-permute-start
  313.1 6.3 collective-permute-start
  323.2 6.3 collective-permute-start
  333.3 6.3 collective-permute-start
  339.6 3.1 collective-permute-done
  343.7 6.7 collective-permute-start
  350.4 4.0 collective-permute-done
  355.3 6.4 collective-permute-start
  361.7 3.0 collective-permute-done
  365.6 6.2 collective-permute-start
  375.6 6.2 collective-permute-start
  385.5 6.4 collective-permute-start
  395.7 6.3 collective-permute-start
  405.8 6.3 collective-permute-start
  414.9 7.7 %while.36 = (s32[]{:T(128)}, f32[2,128,128]{2,1,0:T(8,128)S(1)}, f32[4,2,128,128]{3,2,1,0:T(8,128)}, f32[4,2,128,128]{3,2,1,0:T(8,128)}, f32[4,2,128,128]{3,2,1,0:T(8,128)}, /*index=5*/s32[]{:T(128)}) while((s32[]{:T(128)}, f32[2,128,128]{2,1,0:T(8,128)S(1)}, f32[4,2,128,128]{3,2,1,0:T(8,128)}, f32[4,2,128,128]{3,2,1,0:T(8,128)}, ...), condition=%wide.region_10.11_spmd, body=%wide.region_9.10_spmd.sunk | while | flops 50364416 | bytes 1049681 | solution.py:132
  431.1 79.2 %reduce-scatter.3.cloned.1.call-done = bf16[32,2048]{1,0:T(8,128)(2,1)} async-done(((bf16[256,2048]{1,0:T(8,128)(2,1)}), bf16[32,2048]{1,0:T(8,128)(2,1)}) %reduce-scatter.3.cloned.1.call-update) | async-done | bytes 131088 | tf_op jit(solution)/shard_map/reduce_scatter | solution.py:169
  518.5 3.2 fusion.16
  521.8 19.7 %all-gather.2.cloned.1.call-done = bf16[256,2048]{1,0:T(8,128)(2,1)} async-done(((bf16[32,2048]{1,0:T(8,128)(2,1)}), bf16[256,2048]{1,0:T(8,128)(2,1)}) %all-gather.2.cloned.1.call-update) | async-done | bytes 1048592 | tf_op jit(solution)/shard_map/all_gather | solution.py:180
  541.6 3.1 convolution_convert_fusion
  546.9 143.2 %psum.15 = bf16[4,3,3,256]{3,0,2,1:T(4,128)(2,1)} all-reduce(bf16[4,3,3,256]{3,0,2,1:T(4,128)(2,1)} %convolution_convert_fusion.2), channel_id=1, replica_groups=mesh['seq'=32,'win'=4,'wout'=2] {'seq'}, use_global_device_ids=true, to_apply=%region_18.19 | all-reduce | flops 9216 | bytes 36864 | tf_op jit(solution)/shard_map/psum | solution.py:160
  (195 shorter events, 179.8 us)
Async XLA Ops:
  8.0 533.6 %copy-start = (bf16[512,3072]{1,0:T(8,128)(2,1)S(1)}, bf16[512,3072]{1,0:T(8,128)(2,1)}, u32[]{:S(2)}) copy-start(bf16[512,3072]{1,0:T(8,128)(2,1)} %param.23) | copy-start | bytes 9437188
  8.0 502.3 %reduce-scatter.3.cloned.1.call-start = ((), (), s32[]{:S(2)}) async-start(), calls=%async_computation.2 | async-start | bytes 1179648 | tf_op jit(solution)/shard_map/reduce_scatter | solution.py:169
  8.9 12.8 %collective-permute-start.1 = (bf16[3,3,256]{2,0,1:T(4,128)(2,1)S(1)}, bf16[3,3,256]{2,0,1:T(4,128)(2,1)S(1)}, u32[]{:S(2)}, u32[]{:S(2)}) collective-permute-start(bf16[3,3,256]{2,0,1:T(4,128)(2,1)S(1)} %slice.63), channel_id=1, source_target_pairs={{0,8},{8,16},{16,24},{24,32},{32,40},{40,48},{48,56},{56,64},{64,7... | collective-permute-start | bytes 13832 | tf_op jit(solution)/shard_map/ppermute | solution.py:15
  12.5 4.0 copy-start.8
  13.3 3.9 copy-start.12
  43.4 52.3 %copy-start.1 = (f32[4,64,2,128]{3,1,2,0:T(8,128)}, f32[4,64,2,128]{3,1,2,0:T(8,128)S(1)}, u32[]{:S(2)}) copy-start(f32[4,64,2,128]{3,1,2,0:T(8,128)S(1)} %get-tuple-element.164) | copy-start | bytes 786436
  86.3 9.3 %copy-start.5 = (f32[128,128]{1,0:T(8,128)S(1)}, f32[128,128]{1,0:T(8,128)}, u32[]{:S(2)}) copy-start(f32[128,128]{1,0:T(8,128)} %fusion.63) | copy-start | bytes 196612
  88.1 10.0 %copy-start.3 = (f32[4,2,64,256]{3,2,1,0:T(8,128)}, f32[4,2,64,256]{3,2,1,0:T(8,128)S(1)}, u32[]{:S(2)}) copy-start(f32[4,2,64,256]{3,2,1,0:T(8,128)S(1)} %fusion.28) | copy-start | bytes 1572868
  109.0 6.2 collective-permute-start
  116.2 7.1 %collective-permute-start = (f32[2,128,128]{2,1,0:T(8,128)}, f32[2,128,128]{2,1,0:T(8,128)S(1)}, u32[]{:S(2)}, u32[]{:S(2)}) collective-permute-start(f32[2,128,128]{2,1,0:T(8,128)} %convolution_add_fusion.8), channel_id=1, source_target_pairs={{0,8},{8,16},{16,24},{24,32},{32,40},{40,48},{48,56},{56,64},{64,7... | collective-permute-start | bytes 393224 | tf_op jit(solution)/shard_map/while/body/eval_jaxpr/ppermute | solution.py:15
  124.2 7.1 %collective-permute-start = (f32[2,128,128]{2,1,0:T(8,128)}, f32[2,128,128]{2,1,0:T(8,128)S(1)}, u32[]{:S(2)}, u32[]{:S(2)}) collective-permute-start(f32[2,128,128]{2,1,0:T(8,128)} %convolution_add_fusion.8), channel_id=1, source_target_pairs={{0,8},{8,16},{16,24},{24,32},{32,40},{40,48},{48,56},{56,64},{64,7... | collective-permute-start | bytes 393224 | tf_op jit(solution)/shard_map/while/body/eval_jaxpr/ppermute | solution.py:15
  132.2 7.1 %collective-permute-start = (f32[2,128,128]{2,1,0:T(8,128)}, f32[2,128,128]{2,1,0:T(8,128)S(1)}, u32[]{:S(2)}, u32[]{:S(2)}) collective-permute-start(f32[2,128,128]{2,1,0:T(8,128)} %convolution_add_fusion.8), channel_id=1, source_target_pairs={{0,8},{8,16},{16,24},{24,32},{32,40},{40,48},{48,56},{56,64},{64,7... | collective-permute-start | bytes 393224 | tf_op jit(solution)/shard_map/while/body/eval_jaxpr/ppermute | solution.py:15
  140.1 7.1 %collective-permute-start = (f32[2,128,128]{2,1,0:T(8,128)}, f32[2,128,128]{2,1,0:T(8,128)S(1)}, u32[]{:S(2)}, u32[]{:S(2)}) collective-permute-start(f32[2,128,128]{2,1,0:T(8,128)} %convolution_add_fusion.8), channel_id=1, source_target_pairs={{0,8},{8,16},{16,24},{24,32},{32,40},{40,48},{48,56},{56,64},{64,7... | collective-permute-start | bytes 393224 | tf_op jit(solution)/shard_map/while/body/eval_jaxpr/ppermute | solution.py:15
  148.1 8.8 %collective-permute-start = (f32[2,128,128]{2,1,0:T(8,128)}, f32[2,128,128]{2,1,0:T(8,128)S(1)}, u32[]{:S(2)}, u32[]{:S(2)}) collective-permute-start(f32[2,128,128]{2,1,0:T(8,128)} %convolution_add_fusion.8), channel_id=1, source_target_pairs={{0,8},{8,16},{16,24},{24,32},{32,40},{40,48},{48,56},{56,64},{64,7... | collective-permute-start | bytes 393224 | tf_op jit(solution)/shard_map/while/body/eval_jaxpr/ppermute | solution.py:15
  157.8 9.2 %collective-permute-start = (f32[2,128,128]{2,1,0:T(8,128)}, f32[2,128,128]{2,1,0:T(8,128)S(1)}, u32[]{:S(2)}, u32[]{:S(2)}) collective-permute-start(f32[2,128,128]{2,1,0:T(8,128)} %convolution_add_fusion.8), channel_id=1, source_target_pairs={{0,8},{8,16},{16,24},{24,32},{32,40},{40,48},{48,56},{56,64},{64,7... | collective-permute-start | bytes 393224 | tf_op jit(solution)/shard_map/while/body/eval_jaxpr/ppermute | solution.py:15
  167.9 10.3 %collective-permute-start = (f32[2,128,128]{2,1,0:T(8,128)}, f32[2,128,128]{2,1,0:T(8,128)S(1)}, u32[]{:S(2)}, u32[]{:S(2)}) collective-permute-start(f32[2,128,128]{2,1,0:T(8,128)} %convolution_add_fusion.8), channel_id=1, source_target_pairs={{0,8},{8,16},{16,24},{24,32},{32,40},{40,48},{48,56},{56,64},{64,7... | collective-permute-start | bytes 393224 | tf_op jit(solution)/shard_map/while/body/eval_jaxpr/ppermute | solution.py:15
  179.2 10.4 %collective-permute-start = (f32[2,128,128]{2,1,0:T(8,128)}, f32[2,128,128]{2,1,0:T(8,128)S(1)}, u32[]{:S(2)}, u32[]{:S(2)}) collective-permute-start(f32[2,128,128]{2,1,0:T(8,128)} %convolution_add_fusion.8), channel_id=1, source_target_pairs={{0,8},{8,16},{16,24},{24,32},{32,40},{40,48},{48,56},{56,64},{64,7... | collective-permute-start | bytes 393224 | tf_op jit(solution)/shard_map/while/body/eval_jaxpr/ppermute | solution.py:15
  190.5 8.9 %collective-permute-start = (f32[2,128,128]{2,1,0:T(8,128)}, f32[2,128,128]{2,1,0:T(8,128)S(1)}, u32[]{:S(2)}, u32[]{:S(2)}) collective-permute-start(f32[2,128,128]{2,1,0:T(8,128)} %convolution_add_fusion.8), channel_id=1, source_target_pairs={{0,8},{8,16},{16,24},{24,32},{32,40},{40,48},{48,56},{56,64},{64,7... | collective-permute-start | bytes 393224 | tf_op jit(solution)/shard_map/while/body/eval_jaxpr/ppermute | solution.py:15
  200.3 8.7 %collective-permute-start = (f32[2,128,128]{2,1,0:T(8,128)}, f32[2,128,128]{2,1,0:T(8,128)S(1)}, u32[]{:S(2)}, u32[]{:S(2)}) collective-permute-start(f32[2,128,128]{2,1,0:T(8,128)} %convolution_add_fusion.8), channel_id=1, source_target_pairs={{0,8},{8,16},{16,24},{24,32},{32,40},{40,48},{48,56},{56,64},{64,7... | collective-permute-start | bytes 393224 | tf_op jit(solution)/shard_map/while/body/eval_jaxpr/ppermute | solution.py:15
  210.0 9.2 %collective-permute-start = (f32[2,128,128]{2,1,0:T(8,128)}, f32[2,128,128]{2,1,0:T(8,128)S(1)}, u32[]{:S(2)}, u32[]{:S(2)}) collective-permute-start(f32[2,128,128]{2,1,0:T(8,128)} %convolution_add_fusion.8), channel_id=1, source_target_pairs={{0,8},{8,16},{16,24},{24,32},{32,40},{40,48},{48,56},{56,64},{64,7... | collective-permute-start | bytes 393224 | tf_op jit(solution)/shard_map/while/body/eval_jaxpr/ppermute | solution.py:15
  220.1 9.2 %collective-permute-start = (f32[2,128,128]{2,1,0:T(8,128)}, f32[2,128,128]{2,1,0:T(8,128)S(1)}, u32[]{:S(2)}, u32[]{:S(2)}) collective-permute-start(f32[2,128,128]{2,1,0:T(8,128)} %convolution_add_fusion.8), channel_id=1, source_target_pairs={{0,8},{8,16},{16,24},{24,32},{32,40},{40,48},{48,56},{56,64},{64,7... | collective-permute-start | bytes 393224 | tf_op jit(solution)/shard_map/while/body/eval_jaxpr/ppermute | solution.py:15
  230.3 9.2 %collective-permute-start = (f32[2,128,128]{2,1,0:T(8,128)}, f32[2,128,128]{2,1,0:T(8,128)S(1)}, u32[]{:S(2)}, u32[]{:S(2)}) collective-permute-start(f32[2,128,128]{2,1,0:T(8,128)} %convolution_add_fusion.8), channel_id=1, source_target_pairs={{0,8},{8,16},{16,24},{24,32},{32,40},{40,48},{48,56},{56,64},{64,7... | collective-permute-start | bytes 393224 | tf_op jit(solution)/shard_map/while/body/eval_jaxpr/ppermute | solution.py:15
  240.4 9.2 %collective-permute-start = (f32[2,128,128]{2,1,0:T(8,128)}, f32[2,128,128]{2,1,0:T(8,128)S(1)}, u32[]{:S(2)}, u32[]{:S(2)}) collective-permute-start(f32[2,128,128]{2,1,0:T(8,128)} %convolution_add_fusion.8), channel_id=1, source_target_pairs={{0,8},{8,16},{16,24},{24,32},{32,40},{40,48},{48,56},{56,64},{64,7... | collective-permute-start | bytes 393224 | tf_op jit(solution)/shard_map/while/body/eval_jaxpr/ppermute | solution.py:15
  250.5 9.9 %collective-permute-start = (f32[2,128,128]{2,1,0:T(8,128)}, f32[2,128,128]{2,1,0:T(8,128)S(1)}, u32[]{:S(2)}, u32[]{:S(2)}) collective-permute-start(f32[2,128,128]{2,1,0:T(8,128)} %convolution_add_fusion.8), channel_id=1, source_target_pairs={{0,8},{8,16},{16,24},{24,32},{32,40},{40,48},{48,56},{56,64},{64,7... | collective-permute-start | bytes 393224 | tf_op jit(solution)/shard_map/while/body/eval_jaxpr/ppermute | solution.py:15
  261.3 10.4 %collective-permute-start = (f32[2,128,128]{2,1,0:T(8,128)}, f32[2,128,128]{2,1,0:T(8,128)S(1)}, u32[]{:S(2)}, u32[]{:S(2)}) collective-permute-start(f32[2,128,128]{2,1,0:T(8,128)} %convolution_add_fusion.8), channel_id=1, source_target_pairs={{0,8},{8,16},{16,24},{24,32},{32,40},{40,48},{48,56},{56,64},{64,7... | collective-permute-start | bytes 393224 | tf_op jit(solution)/shard_map/while/body/eval_jaxpr/ppermute | solution.py:15
  272.6 9.5 %collective-permute-start = (f32[2,128,128]{2,1,0:T(8,128)}, f32[2,128,128]{2,1,0:T(8,128)S(1)}, u32[]{:S(2)}, u32[]{:S(2)}) collective-permute-start(f32[2,128,128]{2,1,0:T(8,128)} %convolution_add_fusion.8), channel_id=1, source_target_pairs={{0,8},{8,16},{16,24},{24,32},{32,40},{40,48},{48,56},{56,64},{64,7... | collective-permute-start | bytes 393224 | tf_op jit(solution)/shard_map/while/body/eval_jaxpr/ppermute | solution.py:15
  283.0 8.8 %collective-permute-start = (f32[2,128,128]{2,1,0:T(8,128)}, f32[2,128,128]{2,1,0:T(8,128)S(1)}, u32[]{:S(2)}, u32[]{:S(2)}) collective-permute-start(f32[2,128,128]{2,1,0:T(8,128)} %convolution_add_fusion.8), channel_id=1, source_target_pairs={{0,8},{8,16},{16,24},{24,32},{32,40},{40,48},{48,56},{56,64},{64,7... | collective-permute-start | bytes 393224 | tf_op jit(solution)/shard_map/while/body/eval_jaxpr/ppermute | solution.py:15
  292.8 9.2 %collective-permute-start = (f32[2,128,128]{2,1,0:T(8,128)}, f32[2,128,128]{2,1,0:T(8,128)S(1)}, u32[]{:S(2)}, u32[]{:S(2)}) collective-permute-start(f32[2,128,128]{2,1,0:T(8,128)} %convolution_add_fusion.8), channel_id=1, source_target_pairs={{0,8},{8,16},{16,24},{24,32},{32,40},{40,48},{48,56},{56,64},{64,7... | collective-permute-start | bytes 393224 | tf_op jit(solution)/shard_map/while/body/eval_jaxpr/ppermute | solution.py:15
  302.9 9.2 %collective-permute-start = (f32[2,128,128]{2,1,0:T(8,128)}, f32[2,128,128]{2,1,0:T(8,128)S(1)}, u32[]{:S(2)}, u32[]{:S(2)}) collective-permute-start(f32[2,128,128]{2,1,0:T(8,128)} %convolution_add_fusion.8), channel_id=1, source_target_pairs={{0,8},{8,16},{16,24},{24,32},{32,40},{40,48},{48,56},{56,64},{64,7... | collective-permute-start | bytes 393224 | tf_op jit(solution)/shard_map/while/body/eval_jaxpr/ppermute | solution.py:15
  313.1 9.2 %collective-permute-start = (f32[2,128,128]{2,1,0:T(8,128)}, f32[2,128,128]{2,1,0:T(8,128)S(1)}, u32[]{:S(2)}, u32[]{:S(2)}) collective-permute-start(f32[2,128,128]{2,1,0:T(8,128)} %convolution_add_fusion.8), channel_id=1, source_target_pairs={{0,8},{8,16},{16,24},{24,32},{32,40},{40,48},{48,56},{56,64},{64,7... | collective-permute-start | bytes 393224 | tf_op jit(solution)/shard_map/while/body/eval_jaxpr/ppermute | solution.py:15
  323.2 9.2 %collective-permute-start = (f32[2,128,128]{2,1,0:T(8,128)}, f32[2,128,128]{2,1,0:T(8,128)S(1)}, u32[]{:S(2)}, u32[]{:S(2)}) collective-permute-start(f32[2,128,128]{2,1,0:T(8,128)} %convolution_add_fusion.8), channel_id=1, source_target_pairs={{0,8},{8,16},{16,24},{24,32},{32,40},{40,48},{48,56},{56,64},{64,7... | collective-permute-start | bytes 393224 | tf_op jit(solution)/shard_map/while/body/eval_jaxpr/ppermute | solution.py:15
  333.3 9.5 %collective-permute-start = (f32[2,128,128]{2,1,0:T(8,128)}, f32[2,128,128]{2,1,0:T(8,128)S(1)}, u32[]{:S(2)}, u32[]{:S(2)}) collective-permute-start(f32[2,128,128]{2,1,0:T(8,128)} %convolution_add_fusion.8), channel_id=1, source_target_pairs={{0,8},{8,16},{16,24},{24,32},{32,40},{40,48},{48,56},{56,64},{64,7... | collective-permute-start | bytes 393224 | tf_op jit(solution)/shard_map/while/body/eval_jaxpr/ppermute | solution.py:15
  343.7 10.7 %collective-permute-start = (f32[2,128,128]{2,1,0:T(8,128)}, f32[2,128,128]{2,1,0:T(8,128)S(1)}, u32[]{:S(2)}, u32[]{:S(2)}) collective-permute-start(f32[2,128,128]{2,1,0:T(8,128)} %convolution_add_fusion.8), channel_id=1, source_target_pairs={{0,8},{8,16},{16,24},{24,32},{32,40},{40,48},{48,56},{56,64},{64,7... | collective-permute-start | bytes 393224 | tf_op jit(solution)/shard_map/while/body/eval_jaxpr/ppermute | solution.py:15
  355.3 9.4 %collective-permute-start = (f32[2,128,128]{2,1,0:T(8,128)}, f32[2,128,128]{2,1,0:T(8,128)S(1)}, u32[]{:S(2)}, u32[]{:S(2)}) collective-permute-start(f32[2,128,128]{2,1,0:T(8,128)} %convolution_add_fusion.8), channel_id=1, source_target_pairs={{0,8},{8,16},{16,24},{24,32},{32,40},{40,48},{48,56},{56,64},{64,7... | collective-permute-start | bytes 393224 | tf_op jit(solution)/shard_map/while/body/eval_jaxpr/ppermute | solution.py:15
  365.6 9.1 %collective-permute-start = (f32[2,128,128]{2,1,0:T(8,128)}, f32[2,128,128]{2,1,0:T(8,128)S(1)}, u32[]{:S(2)}, u32[]{:S(2)}) collective-permute-start(f32[2,128,128]{2,1,0:T(8,128)} %convolution_add_fusion.8), channel_id=1, source_target_pairs={{0,8},{8,16},{16,24},{24,32},{32,40},{40,48},{48,56},{56,64},{64,7... | collective-permute-start | bytes 393224 | tf_op jit(solution)/shard_map/while/body/eval_jaxpr/ppermute | solution.py:15
  375.6 9.0 %collective-permute-start = (f32[2,128,128]{2,1,0:T(8,128)}, f32[2,128,128]{2,1,0:T(8,128)S(1)}, u32[]{:S(2)}, u32[]{:S(2)}) collective-permute-start(f32[2,128,128]{2,1,0:T(8,128)} %convolution_add_fusion.8), channel_id=1, source_target_pairs={{0,8},{8,16},{16,24},{24,32},{32,40},{40,48},{48,56},{56,64},{64,7... | collective-permute-start | bytes 393224 | tf_op jit(solution)/shard_map/while/body/eval_jaxpr/ppermute | solution.py:15
  385.5 9.2 %collective-permute-start = (f32[2,128,128]{2,1,0:T(8,128)}, f32[2,128,128]{2,1,0:T(8,128)S(1)}, u32[]{:S(2)}, u32[]{:S(2)}) collective-permute-start(f32[2,128,128]{2,1,0:T(8,128)} %convolution_add_fusion.8), channel_id=1, source_target_pairs={{0,8},{8,16},{16,24},{24,32},{32,40},{40,48},{48,56},{56,64},{64,7... | collective-permute-start | bytes 393224 | tf_op jit(solution)/shard_map/while/body/eval_jaxpr/ppermute | solution.py:15
  395.7 9.2 %collective-permute-start = (f32[2,128,128]{2,1,0:T(8,128)}, f32[2,128,128]{2,1,0:T(8,128)S(1)}, u32[]{:S(2)}, u32[]{:S(2)}) collective-permute-start(f32[2,128,128]{2,1,0:T(8,128)} %convolution_add_fusion.8), channel_id=1, source_target_pairs={{0,8},{8,16},{16,24},{24,32},{32,40},{40,48},{48,56},{56,64},{64,7... | collective-permute-start | bytes 393224 | tf_op jit(solution)/shard_map/while/body/eval_jaxpr/ppermute | solution.py:15
  405.8 9.2 %collective-permute-start = (f32[2,128,128]{2,1,0:T(8,128)}, f32[2,128,128]{2,1,0:T(8,128)S(1)}, u32[]{:S(2)}, u32[]{:S(2)}) collective-permute-start(f32[2,128,128]{2,1,0:T(8,128)} %convolution_add_fusion.8), channel_id=1, source_target_pairs={{0,8},{8,16},{16,24},{24,32},{32,40},{40,48},{48,56},{56,64},{64,7... | collective-permute-start | bytes 393224 | tf_op jit(solution)/shard_map/while/body/eval_jaxpr/ppermute | solution.py:15
  414.9 7.7 %copy-start.4 = (f32[4,2,64,128]{3,2,1,0:T(8,128)S(1)}, f32[4,2,64,128]{3,2,1,0:T(8,128)}, u32[]{:S(2)}) copy-start(f32[4,2,64,128]{3,2,1,0:T(8,128)} %fusion.56) | copy-start | bytes 786436
  422.7 87.6 %copy-start.6 = (bf16[32,2048]{1,0:T(8,128)(2,1)S(1)}, bf16[32,2048]{1,0:T(8,128)(2,1)}, u32[]{:S(2)}) copy-start(bf16[32,2048]{1,0:T(8,128)(2,1)} %param.21) | copy-start | bytes 393220
  427.1 89.4 %copy-start.2 = (f32[4,64,2,128]{3,1,2,0:T(8,128)S(1)}, f32[4,64,2,128]{3,1,2,0:T(8,128)}, u32[]{:S(2)}) copy-start(f32[4,64,2,128]{3,1,2,0:T(8,128)} %copy-done.1) | copy-start | bytes 786436
  431.0 110.5 %all-gather.2.cloned.1.call-start = ((), (), s32[]{:S(2)}) async-start(), calls=%async_computation.3 | async-start | bytes 1179648 | tf_op jit(solution)/shard_map/all_gather | solution.py:180
  513.1 177.0 %all-reduce.2.cloned.1.call-start = ((), (), s32[]{:S(2)}) async-start(), calls=%async_computation.5 | async-start | bytes 524288 | tf_op jit(solution)/shard_map/psum | solution.py:159
  521.8 24.2 %copy-start.7 = (bf16[256,3,256]{2,0,1:T(8,128)(2,1)S(1)}, bf16[256,3,256]{2,0,1:T(8,128)(2,1)}, u32[]{:S(2)}) copy-start(bf16[256,3,256]{2,0,1:T(8,128)(2,1)} %param.15) | copy-start | bytes 1179652
  521.8 24.2 %copy-start.9 = (s32[259]{0:T(512)S(1)}, s32[259]{0:T(512)}, u32[]{:S(2)}) copy-start(s32[259]{0:T(512)} %copy-done.8) | copy-start | bytes 3112
  521.8 24.2 %copy-start.11 = (bf16[3,3,256]{2,0,1:T(4,128)(2,1)S(1)}, bf16[3,3,256]{2,0,1:T(4,128)(2,1)}, u32[]{:S(2)}) copy-start(bf16[3,3,256]{2,0,1:T(4,128)(2,1)} %copy-done.10) | copy-start | bytes 13828
  521.8 170.1 %reduce-scatter.5.cloned.1.call-start = ((), (), s32[]{:S(2)}) async-start(), calls=%async_computation.4 | async-start | bytes 1966080 | tf_op jit(solution)/shard_map/reduce_scatter | solution.py:182
  (1 other events, 0.6 us)
Sparse Core Ops, SparseCore 0:
  431.2 79.0 reduce-scatter.2
  513.2 28.3 all-gather.1
  544.9 27.9 reduce-scatter.4
Sparse Core Ops, SparseCore 1:
  521.9 147.6 all-reduce.1
where the time goes:
time: 701 us; the launch traced here: 699 us
  waiting for transfers between devices  191 us (27%)
  starting transfers between devices  190 us (27%)
  blocking collectives  143 us (20%)
  matrix products  73.4 us (10%)
  other arithmetic  63.6 us (9%)
  local copies, waits for them, and re-layouts  22.1 us (3%)
  between operations  15.5 us (2%)
    ppermute x32, starting transfers between devices, from_behind(): lax.ppermute(value, axis, [(source, source + steps) for source in range(l...  189 us
    psum x1, blocking collectives, body(): lax.psum(edge_vals.astype(jnp.bfloat16), 'seq').astype(jnp.float32)  143 us
    ppermute x32, waiting for transfers between devices, from_behind(): lax.ppermute(value, axis, [(source, source + steps) for source in range(l...  92 us
    reduce_scatter x1, waiting for transfers between devices, body(): lax.psum_scatter(jnp.dot(normed_heads, w_out, preferred_element_type=jnp....  79.2 us
    dot_general x52, matrix products, outer_product(): return jnp.einsum(form, left, right, precision=lax.Precision.HIGHEST)  63 us
    another operation x4, other arithmetic, body(): lax.linalg.triangular_solve(system, targets, left_side=True, lower=True,...  42 us
    all_gather x1, waiting for transfers between devices, body(): lax.all_gather(normed_stream, ('win', 'wout'), axis=0, tiled=True)  19.7 us
  transfers between devices with their start and end apart: 36, of which 33 were waited for; matrix products, arithmetic and copies ran while one was open for 4% of the time, Pallas kernels for 0%

commit v1 on v0

--- a/solution.py
+++ b/solution.py
@@ -177,7 +177,8 @@
     scale_stream = jnp.sqrt(jnp.mean(summed * summed, axis=-1, keepdims=True) + 1e-05)
     normed_stream = (summed / scale_stream * norm_gain).astype(jnp.bfloat16)
     in_block = w_qkv.shape[0]
-    all_rows = lax.all_gather(normed_stream, ("win", "wout"), axis=0, tiled=True)
+    sent = jnp.stack([normed_stream] * lax.axis_size(("win", "wout")))
+    all_rows = jnp.concatenate(lax.all_to_all(sent, ("win", "wout"), 0, 0), axis=0)
     columns = lax.dynamic_slice_in_dim(all_rows, lax.axis_index("win") * in_block, in_block, 1)
     projected = lax.psum_scatter(
         jnp.dot(columns, w_qkv, preferred_element_type=jnp.float32).astype(jnp.bfloat16),

time: 701 us -> 697 us (level)
  waiting for transfers between devices: 191 us -> 176 us
  starting transfers between devices: 190 us -> 199 us
    all_gather x1 -> x0, waiting for transfers between devices: 19.7 us -> none  [body(): lax.all_gather(normed_stream, ('win', 'wout'), axis=0, tiled=True)]
    all_to_all x0 -> x1, starting transfers between devices: none -> 9.56 us  [body(): lax.all_to_all(sent, ('win', 'wout'), 0, 0)]
where the time goes in v1:
time: 697 us; the launch traced here: 693 us
  starting transfers between devices  199 us (29%)
  waiting for transfers between devices  176 us (25%)
  blocking collectives  143 us (21%)
  matrix products  73.4 us (11%)
  other arithmetic  63.6 us (9%)
  local copies, waits for them, and re-layouts  21.7 us (3%)
  between operations  15.8 us (2%)
    ppermute x32, starting transfers between devices, from_behind(): lax.ppermute(value, axis, [(source, source + steps) for source in range(l...  189 us
    psum x1, blocking collectives, body(): lax.psum(edge_vals.astype(jnp.bfloat16), 'seq').astype(jnp.float32)  143 us
    ppermute x32, waiting for transfers between devices, from_behind(): lax.ppermute(value, axis, [(source, source + steps) for source in range(l...  92 us
    reduce_scatter x1, waiting for transfers between devices, body(): lax.psum_scatter(jnp.dot(normed_heads, w_out, preferred_element_type=jnp....  78 us
    dot_general x52, matrix products, outer_product(): return jnp.einsum(form, left, right, precision=lax.Precision.HIGHEST)  62.9 us
    another operation x4, other arithmetic, body(): lax.linalg.triangular_solve(system, targets, left_side=True, lower=True,...  42 us
  transfers between devices with their start and end apart: 36, of which 33 were waited for; matrix products, arithmetic and copies ran while one was open for 4% of the time, Pallas kernels for 0%

profile of v1, /device:TPU:16, one launch (start us, length us, event | category | flops | bytes accessed | tf_op | source)
XLA Modules:
  0.0 692.8 jit_solution(943529609787550159)
XLA Ops:
  8.9 3.5 collective-permute-start.1
  45.6 40.7 %custom-call.3 = f32[4,2,1,64,64]{3,4,2,1,0:T(8,128)} custom-call(f32[4,2,1,64,64]{4,3,2,1,0:T(8,128)} %fusion.23), custom_call_target="InvertDiagBlocksLowerTriangular" | custom-call | tf_op jit(solution)/shard_map/triangular_solve | solution.py:85
  98.1 9.9 %while.37 = (s32[]{:T(128)}, f32[2,128,128]{2,1,0:T(8,128)S(1)}, f32[2,128,128]{2,1,0:T(8,128)S(1)}, f32[4,2,128,128]{3,2,1,0:T(8,128)}, f32[4,2,128,128]{3,2,1,0:T(8,128)}, /*index=5*/s32[]{:T(128)}, s32[]{:T(128)}) while((s32[]{:T(128)}, f32[2,128,128]{2,1,0:T(8,128)S(1)}, f32[2,128,128]{2,1,0:T(8,128)S(1)}, ...), condition=%wide.region_6.7_spmd.clone, body=%wide.region_5.6_spmd.clone.sunk | while | flops 100728832 | bytes 1443426 | solution.py:116
  108.0 306.8 %while.35 = (s32[]{:T(128)}, f32[2,128,128]{2,1,0:T(8,128)S(1)}, f32[2,128,128]{2,1,0:T(8,128)S(1)}, f32[2,128,128]{2,1,0:T(8,128)S(1)}, s32[]{:T(128)}) while((s32[]{:T(128)}, f32[2,128,128]{2,1,0:T(8,128)S(1)}, f32[2,128,128]{2,1,0:T(8,128)S(1)}, f32[2,128,128]{2,1,0:T(8,128)S(1)}, s32[]{:T(128)}) %tuple.81), condition=%wide.region_8.9_spmd, body=%wide.region_7.8_spmd.sunk | while | flops 50364416 | bytes 1048677 | solution.py:124
  109.0 3.4 collective-permute-start
  116.1 4.2 collective-permute-start
  124.1 4.2 collective-permute-start
  132.1 4.2 collective-permute-start
  140.1 4.2 collective-permute-start
  148.1 6.0 collective-permute-start
  157.8 6.3 collective-permute-start
  167.9 6.5 collective-permute-start
  174.3 3.9 collective-permute-done
  179.1 6.9 %collective-permute-start = (f32[2,128,128]{2,1,0:T(8,128)}, f32[2,128,128]{2,1,0:T(8,128)S(1)}, u32[]{:S(2)}, u32[]{:S(2)}) collective-permute-start(f32[2,128,128]{2,1,0:T(8,128)} %convolution_add_fusion.8), channel_id=1, source_target_pairs={{0,8},{8,16},{16,24},{24,32},{32,40},{40,48},{48,56},{56,64},{64,7... | collective-permute-start | bytes 393224 | tf_op jit(solution)/shard_map/while/body/eval_jaxpr/ppermute | solution.py:15
  186.1 3.4 collective-permute-done
  190.4 6.1 collective-permute-start
  200.3 5.9 collective-permute-start
  209.9 6.4 collective-permute-start
  220.1 6.4 collective-permute-start
  230.2 6.3 collective-permute-start
  240.3 6.3 collective-permute-start
  250.4 6.3 collective-permute-start
  256.8 3.5 collective-permute-done
  261.2 6.7 collective-permute-start
  267.9 3.7 collective-permute-done
  272.5 6.7 collective-permute-start
  283.0 6.0 collective-permute-start
  292.7 6.4 collective-permute-start
  302.9 6.4 collective-permute-start
  313.0 6.3 collective-permute-start
  323.1 6.3 collective-permute-start
  333.2 6.3 collective-permute-start
  339.6 3.1 collective-permute-done
  343.6 6.7 collective-permute-start
  350.3 4.0 collective-permute-done
  355.3 6.4 collective-permute-start
  365.5 6.2 collective-permute-start
  375.5 6.2 collective-permute-start
  385.5 6.4 collective-permute-start
  395.6 6.3 collective-permute-start
  405.7 6.3 collective-permute-start
  414.9 7.7 %while.36 = (s32[]{:T(128)}, f32[2,128,128]{2,1,0:T(8,128)S(1)}, f32[4,2,128,128]{3,2,1,0:T(8,128)}, f32[4,2,128,128]{3,2,1,0:T(8,128)}, f32[4,2,128,128]{3,2,1,0:T(8,128)}, /*index=5*/s32[]{:T(128)}) while((s32[]{:T(128)}, f32[2,128,128]{2,1,0:T(8,128)S(1)}, f32[4,2,128,128]{3,2,1,0:T(8,128)}, f32[4,2,128,128]{3,2,1,0:T(8,128)}, ...), condition=%wide.region_10.11_spmd, body=%wide.region_9.10_spmd.sunk | while | flops 50364416 | bytes 1049681 | solution.py:132
  430.6 78.0 %reduce-scatter.3.cloned.1.call-done = bf16[32,2048]{1,0:T(8,128)(2,1)} async-done(((bf16[256,2048]{1,0:T(8,128)(2,1)}), bf16[32,2048]{1,0:T(8,128)(2,1)}) %reduce-scatter.3.cloned.1.call-update) | async-done | bytes 131088 | tf_op jit(solution)/shard_map/reduce_scatter | solution.py:169
  512.5 9.6 %all-to-all-start = ((bf16[8,32,2048]{2,1,0:T(8,128)(2,1)}), bf16[8,32,2048]{2,1,0:T(8,128)(2,1)}, u32[]{:S(2)}, u32[]{:S(2)}) async-start(bf16[8,32,2048]{2,1,0:T(8,128)(2,1)} %stack.2), calls=%async_computation.1 | async-start | bytes 2097152 | tf_op jit(solution)/shard_map/all_to_all | solution.py:181
  526.1 3.2 fusion.16
  529.4 5.5 all-to-all-done
  534.9 3.1 convolution_convert_fusion
  540.3 143.2 %psum.15 = bf16[4,3,3,256]{3,0,2,1:T(4,128)(2,1)} all-reduce(bf16[4,3,3,256]{3,0,2,1:T(4,128)(2,1)} %convolution_convert_fusion.2), channel_id=1, replica_groups=mesh['seq'=32,'win'=4,'wout'=2] {'seq'}, use_global_device_ids=true, to_apply=%region_18.19 | all-reduce | flops 9216 | bytes 36864 | tf_op jit(solution)/shard_map/psum | solution.py:160
  (197 shorter events, 182.1 us)
Async XLA Ops:
  8.0 526.9 %copy-start = (bf16[512,3072]{1,0:T(8,128)(2,1)S(1)}, bf16[512,3072]{1,0:T(8,128)(2,1)}, u32[]{:S(2)}) copy-start(bf16[512,3072]{1,0:T(8,128)(2,1)} %param.23) | copy-start | bytes 9437188
  8.0 500.7 %reduce-scatter.3.cloned.1.call-start = ((), (), s32[]{:S(2)}) async-start(), calls=%async_computation.3 | async-start | bytes 1179648 | tf_op jit(solution)/shard_map/reduce_scatter | solution.py:169
  8.9 12.7 %collective-permute-start.1 = (bf16[3,3,256]{2,0,1:T(4,128)(2,1)S(1)}, bf16[3,3,256]{2,0,1:T(4,128)(2,1)S(1)}, u32[]{:S(2)}, u32[]{:S(2)}) collective-permute-start(bf16[3,3,256]{2,0,1:T(4,128)(2,1)S(1)} %slice.63), channel_id=1, source_target_pairs={{0,8},{8,16},{16,24},{24,32},{32,40},{40,48},{48,56},{56,64},{64,7... | collective-permute-start | bytes 13832 | tf_op jit(solution)/shard_map/ppermute | solution.py:15
  12.5 4.0 copy-start.8
  43.4 52.2 %copy-start.1 = (f32[4,64,2,128]{3,1,2,0:T(8,128)}, f32[4,64,2,128]{3,1,2,0:T(8,128)S(1)}, u32[]{:S(2)}) copy-start(f32[4,64,2,128]{3,1,2,0:T(8,128)S(1)} %get-tuple-element.164) | copy-start | bytes 786436
  86.3 9.3 %copy-start.5 = (f32[128,128]{1,0:T(8,128)S(1)}, f32[128,128]{1,0:T(8,128)}, u32[]{:S(2)}) copy-start(f32[128,128]{1,0:T(8,128)} %fusion.63) | copy-start | bytes 196612
  88.1 10.0 %copy-start.3 = (f32[4,2,64,256]{3,2,1,0:T(8,128)}, f32[4,2,64,256]{3,2,1,0:T(8,128)S(1)}, u32[]{:S(2)}) copy-start(f32[4,2,64,256]{3,2,1,0:T(8,128)S(1)} %fusion.28) | copy-start | bytes 1572868
  109.0 6.2 collective-permute-start
  116.1 7.1 %collective-permute-start = (f32[2,128,128]{2,1,0:T(8,128)}, f32[2,128,128]{2,1,0:T(8,128)S(1)}, u32[]{:S(2)}, u32[]{:S(2)}) collective-permute-start(f32[2,128,128]{2,1,0:T(8,128)} %convolution_add_fusion.8), channel_id=1, source_target_pairs={{0,8},{8,16},{16,24},{24,32},{32,40},{40,48},{48,56},{56,64},{64,7... | collective-permute-start | bytes 393224 | tf_op jit(solution)/shard_map/while/body/eval_jaxpr/ppermute | solution.py:15
  124.1 7.1 %collective-permute-start = (f32[2,128,128]{2,1,0:T(8,128)}, f32[2,128,128]{2,1,0:T(8,128)S(1)}, u32[]{:S(2)}, u32[]{:S(2)}) collective-permute-start(f32[2,128,128]{2,1,0:T(8,128)} %convolution_add_fusion.8), channel_id=1, source_target_pairs={{0,8},{8,16},{16,24},{24,32},{32,40},{40,48},{48,56},{56,64},{64,7... | collective-permute-start | bytes 393224 | tf_op jit(solution)/shard_map/while/body/eval_jaxpr/ppermute | solution.py:15
  132.1 7.1 %collective-permute-start = (f32[2,128,128]{2,1,0:T(8,128)}, f32[2,128,128]{2,1,0:T(8,128)S(1)}, u32[]{:S(2)}, u32[]{:S(2)}) collective-permute-start(f32[2,128,128]{2,1,0:T(8,128)} %convolution_add_fusion.8), channel_id=1, source_target_pairs={{0,8},{8,16},{16,24},{24,32},{32,40},{40,48},{48,56},{56,64},{64,7... | collective-permute-start | bytes 393224 | tf_op jit(solution)/shard_map/while/body/eval_jaxpr/ppermute | solution.py:15
  140.1 7.1 %collective-permute-start = (f32[2,128,128]{2,1,0:T(8,128)}, f32[2,128,128]{2,1,0:T(8,128)S(1)}, u32[]{:S(2)}, u32[]{:S(2)}) collective-permute-start(f32[2,128,128]{2,1,0:T(8,128)} %convolution_add_fusion.8), channel_id=1, source_target_pairs={{0,8},{8,16},{16,24},{24,32},{32,40},{40,48},{48,56},{56,64},{64,7... | collective-permute-start | bytes 393224 | tf_op jit(solution)/shard_map/while/body/eval_jaxpr/ppermute | solution.py:15
  148.1 8.8 %collective-permute-start = (f32[2,128,128]{2,1,0:T(8,128)}, f32[2,128,128]{2,1,0:T(8,128)S(1)}, u32[]{:S(2)}, u32[]{:S(2)}) collective-permute-start(f32[2,128,128]{2,1,0:T(8,128)} %convolution_add_fusion.8), channel_id=1, source_target_pairs={{0,8},{8,16},{16,24},{24,32},{32,40},{40,48},{48,56},{56,64},{64,7... | collective-permute-start | bytes 393224 | tf_op jit(solution)/shard_map/while/body/eval_jaxpr/ppermute | solution.py:15
  157.8 9.2 %collective-permute-start = (f32[2,128,128]{2,1,0:T(8,128)}, f32[2,128,128]{2,1,0:T(8,128)S(1)}, u32[]{:S(2)}, u32[]{:S(2)}) collective-permute-start(f32[2,128,128]{2,1,0:T(8,128)} %convolution_add_fusion.8), channel_id=1, source_target_pairs={{0,8},{8,16},{16,24},{24,32},{32,40},{40,48},{48,56},{56,64},{64,7... | collective-permute-start | bytes 393224 | tf_op jit(solution)/shard_map/while/body/eval_jaxpr/ppermute | solution.py:15
  167.9 10.3 %collective-permute-start = (f32[2,128,128]{2,1,0:T(8,128)}, f32[2,128,128]{2,1,0:T(8,128)S(1)}, u32[]{:S(2)}, u32[]{:S(2)}) collective-permute-start(f32[2,128,128]{2,1,0:T(8,128)} %convolution_add_fusion.8), channel_id=1, source_target_pairs={{0,8},{8,16},{16,24},{24,32},{32,40},{40,48},{48,56},{56,64},{64,7... | collective-permute-start | bytes 393224 | tf_op jit(solution)/shard_map/while/body/eval_jaxpr/ppermute | solution.py:15
  179.1 10.4 %collective-permute-start = (f32[2,128,128]{2,1,0:T(8,128)}, f32[2,128,128]{2,1,0:T(8,128)S(1)}, u32[]{:S(2)}, u32[]{:S(2)}) collective-permute-start(f32[2,128,128]{2,1,0:T(8,128)} %convolution_add_fusion.8), channel_id=1, source_target_pairs={{0,8},{8,16},{16,24},{24,32},{32,40},{40,48},{48,56},{56,64},{64,7... | collective-permute-start | bytes 393224 | tf_op jit(solution)/shard_map/while/body/eval_jaxpr/ppermute | solution.py:15
  190.4 9.0 %collective-permute-start = (f32[2,128,128]{2,1,0:T(8,128)}, f32[2,128,128]{2,1,0:T(8,128)S(1)}, u32[]{:S(2)}, u32[]{:S(2)}) collective-permute-start(f32[2,128,128]{2,1,0:T(8,128)} %convolution_add_fusion.8), channel_id=1, source_target_pairs={{0,8},{8,16},{16,24},{24,32},{32,40},{40,48},{48,56},{56,64},{64,7... | collective-permute-start | bytes 393224 | tf_op jit(solution)/shard_map/while/body/eval_jaxpr/ppermute | solution.py:15
  200.3 8.7 %collective-permute-start = (f32[2,128,128]{2,1,0:T(8,128)}, f32[2,128,128]{2,1,0:T(8,128)S(1)}, u32[]{:S(2)}, u32[]{:S(2)}) collective-permute-start(f32[2,128,128]{2,1,0:T(8,128)} %convolution_add_fusion.8), channel_id=1, source_target_pairs={{0,8},{8,16},{16,24},{24,32},{32,40},{40,48},{48,56},{56,64},{64,7... | collective-permute-start | bytes 393224 | tf_op jit(solution)/shard_map/while/body/eval_jaxpr/ppermute | solution.py:15
  209.9 9.2 %collective-permute-start = (f32[2,128,128]{2,1,0:T(8,128)}, f32[2,128,128]{2,1,0:T(8,128)S(1)}, u32[]{:S(2)}, u32[]{:S(2)}) collective-permute-start(f32[2,128,128]{2,1,0:T(8,128)} %convolution_add_fusion.8), channel_id=1, source_target_pairs={{0,8},{8,16},{16,24},{24,32},{32,40},{40,48},{48,56},{56,64},{64,7... | collective-permute-start | bytes 393224 | tf_op jit(solution)/shard_map/while/body/eval_jaxpr/ppermute | solution.py:15
  220.1 9.2 %collective-permute-start = (f32[2,128,128]{2,1,0:T(8,128)}, f32[2,128,128]{2,1,0:T(8,128)S(1)}, u32[]{:S(2)}, u32[]{:S(2)}) collective-permute-start(f32[2,128,128]{2,1,0:T(8,128)} %convolution_add_fusion.8), channel_id=1, source_target_pairs={{0,8},{8,16},{16,24},{24,32},{32,40},{40,48},{48,56},{56,64},{64,7... | collective-permute-start | bytes 393224 | tf_op jit(solution)/shard_map/while/body/eval_jaxpr/ppermute | solution.py:15
  230.2 9.2 %collective-permute-start = (f32[2,128,128]{2,1,0:T(8,128)}, f32[2,128,128]{2,1,0:T(8,128)S(1)}, u32[]{:S(2)}, u32[]{:S(2)}) collective-permute-start(f32[2,128,128]{2,1,0:T(8,128)} %convolution_add_fusion.8), channel_id=1, source_target_pairs={{0,8},{8,16},{16,24},{24,32},{32,40},{40,48},{48,56},{56,64},{64,7... | collective-permute-start | bytes 393224 | tf_op jit(solution)/shard_map/while/body/eval_jaxpr/ppermute | solution.py:15
  240.3 9.2 %collective-permute-start = (f32[2,128,128]{2,1,0:T(8,128)}, f32[2,128,128]{2,1,0:T(8,128)S(1)}, u32[]{:S(2)}, u32[]{:S(2)}) collective-permute-start(f32[2,128,128]{2,1,0:T(8,128)} %convolution_add_fusion.8), channel_id=1, source_target_pairs={{0,8},{8,16},{16,24},{24,32},{32,40},{40,48},{48,56},{56,64},{64,7... | collective-permute-start | bytes 393224 | tf_op jit(solution)/shard_map/while/body/eval_jaxpr/ppermute | solution.py:15
  250.4 9.9 %collective-permute-start = (f32[2,128,128]{2,1,0:T(8,128)}, f32[2,128,128]{2,1,0:T(8,128)S(1)}, u32[]{:S(2)}, u32[]{:S(2)}) collective-permute-start(f32[2,128,128]{2,1,0:T(8,128)} %convolution_add_fusion.8), channel_id=1, source_target_pairs={{0,8},{8,16},{16,24},{24,32},{32,40},{40,48},{48,56},{56,64},{64,7... | collective-permute-start | bytes 393224 | tf_op jit(solution)/shard_map/while/body/eval_jaxpr/ppermute | solution.py:15
  261.2 10.4 %collective-permute-start = (f32[2,128,128]{2,1,0:T(8,128)}, f32[2,128,128]{2,1,0:T(8,128)S(1)}, u32[]{:S(2)}, u32[]{:S(2)}) collective-permute-start(f32[2,128,128]{2,1,0:T(8,128)} %convolution_add_fusion.8), channel_id=1, source_target_pairs={{0,8},{8,16},{16,24},{24,32},{32,40},{40,48},{48,56},{56,64},{64,7... | collective-permute-start | bytes 393224 | tf_op jit(solution)/shard_map/while/body/eval_jaxpr/ppermute | solution.py:15
  272.5 9.5 %collective-permute-start = (f32[2,128,128]{2,1,0:T(8,128)}, f32[2,128,128]{2,1,0:T(8,128)S(1)}, u32[]{:S(2)}, u32[]{:S(2)}) collective-permute-start(f32[2,128,128]{2,1,0:T(8,128)} %convolution_add_fusion.8), channel_id=1, source_target_pairs={{0,8},{8,16},{16,24},{24,32},{32,40},{40,48},{48,56},{56,64},{64,7... | collective-permute-start | bytes 393224 | tf_op jit(solution)/shard_map/while/body/eval_jaxpr/ppermute | solution.py:15
  283.0 8.8 %collective-permute-start = (f32[2,128,128]{2,1,0:T(8,128)}, f32[2,128,128]{2,1,0:T(8,128)S(1)}, u32[]{:S(2)}, u32[]{:S(2)}) collective-permute-start(f32[2,128,128]{2,1,0:T(8,128)} %convolution_add_fusion.8), channel_id=1, source_target_pairs={{0,8},{8,16},{16,24},{24,32},{32,40},{40,48},{48,56},{56,64},{64,7... | collective-permute-start | bytes 393224 | tf_op jit(solution)/shard_map/while/body/eval_jaxpr/ppermute | solution.py:15
  292.7 9.2 %collective-permute-start = (f32[2,128,128]{2,1,0:T(8,128)}, f32[2,128,128]{2,1,0:T(8,128)S(1)}, u32[]{:S(2)}, u32[]{:S(2)}) collective-permute-start(f32[2,128,128]{2,1,0:T(8,128)} %convolution_add_fusion.8), channel_id=1, source_target_pairs={{0,8},{8,16},{16,24},{24,32},{32,40},{40,48},{48,56},{56,64},{64,7... | collective-permute-start | bytes 393224 | tf_op jit(solution)/shard_map/while/body/eval_jaxpr/ppermute | solution.py:15
  302.9 9.2 %collective-permute-start = (f32[2,128,128]{2,1,0:T(8,128)}, f32[2,128,128]{2,1,0:T(8,128)S(1)}, u32[]{:S(2)}, u32[]{:S(2)}) collective-permute-start(f32[2,128,128]{2,1,0:T(8,128)} %convolution_add_fusion.8), channel_id=1, source_target_pairs={{0,8},{8,16},{16,24},{24,32},{32,40},{40,48},{48,56},{56,64},{64,7... | collective-permute-start | bytes 393224 | tf_op jit(solution)/shard_map/while/body/eval_jaxpr/ppermute | solution.py:15
  313.0 9.2 %collective-permute-start = (f32[2,128,128]{2,1,0:T(8,128)}, f32[2,128,128]{2,1,0:T(8,128)S(1)}, u32[]{:S(2)}, u32[]{:S(2)}) collective-permute-start(f32[2,128,128]{2,1,0:T(8,128)} %convolution_add_fusion.8), channel_id=1, source_target_pairs={{0,8},{8,16},{16,24},{24,32},{32,40},{40,48},{48,56},{56,64},{64,7... | collective-permute-start | bytes 393224 | tf_op jit(solution)/shard_map/while/body/eval_jaxpr/ppermute | solution.py:15
  323.1 9.2 %collective-permute-start = (f32[2,128,128]{2,1,0:T(8,128)}, f32[2,128,128]{2,1,0:T(8,128)S(1)}, u32[]{:S(2)}, u32[]{:S(2)}) collective-permute-start(f32[2,128,128]{2,1,0:T(8,128)} %convolution_add_fusion.8), channel_id=1, source_target_pairs={{0,8},{8,16},{16,24},{24,32},{32,40},{40,48},{48,56},{56,64},{64,7... | collective-permute-start | bytes 393224 | tf_op jit(solution)/shard_map/while/body/eval_jaxpr/ppermute | solution.py:15
  333.2 9.5 %collective-permute-start = (f32[2,128,128]{2,1,0:T(8,128)}, f32[2,128,128]{2,1,0:T(8,128)S(1)}, u32[]{:S(2)}, u32[]{:S(2)}) collective-permute-start(f32[2,128,128]{2,1,0:T(8,128)} %convolution_add_fusion.8), channel_id=1, source_target_pairs={{0,8},{8,16},{16,24},{24,32},{32,40},{40,48},{48,56},{56,64},{64,7... | collective-permute-start | bytes 393224 | tf_op jit(solution)/shard_map/while/body/eval_jaxpr/ppermute | solution.py:15
  343.6 10.7 %collective-permute-start = (f32[2,128,128]{2,1,0:T(8,128)}, f32[2,128,128]{2,1,0:T(8,128)S(1)}, u32[]{:S(2)}, u32[]{:S(2)}) collective-permute-start(f32[2,128,128]{2,1,0:T(8,128)} %convolution_add_fusion.8), channel_id=1, source_target_pairs={{0,8},{8,16},{16,24},{24,32},{32,40},{40,48},{48,56},{56,64},{64,7... | collective-permute-start | bytes 393224 | tf_op jit(solution)/shard_map/while/body/eval_jaxpr/ppermute | solution.py:15
  355.3 9.4 %collective-permute-start = (f32[2,128,128]{2,1,0:T(8,128)}, f32[2,128,128]{2,1,0:T(8,128)S(1)}, u32[]{:S(2)}, u32[]{:S(2)}) collective-permute-start(f32[2,128,128]{2,1,0:T(8,128)} %convolution_add_fusion.8), channel_id=1, source_target_pairs={{0,8},{8,16},{16,24},{24,32},{32,40},{40,48},{48,56},{56,64},{64,7... | collective-permute-start | bytes 393224 | tf_op jit(solution)/shard_map/while/body/eval_jaxpr/ppermute | solution.py:15
  365.5 9.1 %collective-permute-start = (f32[2,128,128]{2,1,0:T(8,128)}, f32[2,128,128]{2,1,0:T(8,128)S(1)}, u32[]{:S(2)}, u32[]{:S(2)}) collective-permute-start(f32[2,128,128]{2,1,0:T(8,128)} %convolution_add_fusion.8), channel_id=1, source_target_pairs={{0,8},{8,16},{16,24},{24,32},{32,40},{40,48},{48,56},{56,64},{64,7... | collective-permute-start | bytes 393224 | tf_op jit(solution)/shard_map/while/body/eval_jaxpr/ppermute | solution.py:15
  375.5 9.0 %collective-permute-start = (f32[2,128,128]{2,1,0:T(8,128)}, f32[2,128,128]{2,1,0:T(8,128)S(1)}, u32[]{:S(2)}, u32[]{:S(2)}) collective-permute-start(f32[2,128,128]{2,1,0:T(8,128)} %convolution_add_fusion.8), channel_id=1, source_target_pairs={{0,8},{8,16},{16,24},{24,32},{32,40},{40,48},{48,56},{56,64},{64,7... | collective-permute-start | bytes 393224 | tf_op jit(solution)/shard_map/while/body/eval_jaxpr/ppermute | solution.py:15
  385.5 9.2 %collective-permute-start = (f32[2,128,128]{2,1,0:T(8,128)}, f32[2,128,128]{2,1,0:T(8,128)S(1)}, u32[]{:S(2)}, u32[]{:S(2)}) collective-permute-start(f32[2,128,128]{2,1,0:T(8,128)} %convolution_add_fusion.8), channel_id=1, source_target_pairs={{0,8},{8,16},{16,24},{24,32},{32,40},{40,48},{48,56},{56,64},{64,7... | collective-permute-start | bytes 393224 | tf_op jit(solution)/shard_map/while/body/eval_jaxpr/ppermute | solution.py:15
  395.6 9.2 %collective-permute-start = (f32[2,128,128]{2,1,0:T(8,128)}, f32[2,128,128]{2,1,0:T(8,128)S(1)}, u32[]{:S(2)}, u32[]{:S(2)}) collective-permute-start(f32[2,128,128]{2,1,0:T(8,128)} %convolution_add_fusion.8), channel_id=1, source_target_pairs={{0,8},{8,16},{16,24},{24,32},{32,40},{40,48},{48,56},{56,64},{64,7... | collective-permute-start | bytes 393224 | tf_op jit(solution)/shard_map/while/body/eval_jaxpr/ppermute | solution.py:15
  405.7 9.2 %collective-permute-start = (f32[2,128,128]{2,1,0:T(8,128)}, f32[2,128,128]{2,1,0:T(8,128)S(1)}, u32[]{:S(2)}, u32[]{:S(2)}) collective-permute-start(f32[2,128,128]{2,1,0:T(8,128)} %convolution_add_fusion.8), channel_id=1, source_target_pairs={{0,8},{8,16},{16,24},{24,32},{32,40},{40,48},{48,56},{56,64},{64,7... | collective-permute-start | bytes 393224 | tf_op jit(solution)/shard_map/while/body/eval_jaxpr/ppermute | solution.py:15
  414.9 7.8 %copy-start.4 = (f32[4,2,64,128]{3,2,1,0:T(8,128)S(1)}, f32[4,2,64,128]{3,2,1,0:T(8,128)}, u32[]{:S(2)}) copy-start(f32[4,2,64,128]{3,2,1,0:T(8,128)} %fusion.56) | copy-start | bytes 786436
  422.6 86.1 %copy-start.6 = (bf16[32,2048]{1,0:T(8,128)(2,1)S(1)}, bf16[32,2048]{1,0:T(8,128)(2,1)}, u32[]{:S(2)}) copy-start(bf16[32,2048]{1,0:T(8,128)(2,1)} %param.21) | copy-start | bytes 393220
  429.4 94.8 %copy-start.2 = (f32[4,64,2,128]{3,1,2,0:T(8,128)S(1)}, f32[4,64,2,128]{3,1,2,0:T(8,128)}, u32[]{:S(2)}) copy-start(f32[4,64,2,128]{3,1,2,0:T(8,128)} %copy-done.1) | copy-start | bytes 786436
  511.4 10.7 %copy-start.13 = (s32[4]{0:T(128)S(1)}, s32[4]{0:T(128)}, u32[]{:S(2)}) copy-start(s32[4]{0:T(128)} %get-tuple-element.184) | copy-start | bytes 52
  512.5 22.4 %all-to-all-start = ((bf16[8,32,2048]{2,1,0:T(8,128)(2,1)}), bf16[8,32,2048]{2,1,0:T(8,128)(2,1)}, u32[]{:S(2)}, u32[]{:S(2)}) async-start(bf16[8,32,2048]{2,1,0:T(8,128)(2,1)} %stack.2), calls=%async_computation.1 | async-start | bytes 2097152 | tf_op jit(solution)/shard_map/all_to_all | solution.py:181
  522.0 161.6 %all-reduce.2.cloned.1.call-start = ((), (), s32[]{:S(2)}) async-start(), calls=%async_computation.5 | async-start | bytes 524288 | tf_op jit(solution)/shard_map/psum | solution.py:159
  529.4 156.0 %reduce-scatter.5.cloned.1.call-start = ((), (), s32[]{:S(2)}) async-start(), calls=%async_computation.4 | async-start | bytes 1966080 | tf_op jit(solution)/shard_map/reduce_scatter | solution.py:183
  534.9 4.5 copy-start.7
  534.9 4.5 copy-start.9
  534.9 4.6 copy-start.11
  (2 other events, 4.5 us)
Sparse Core Ops, SparseCore 0:
  429.5 79.1 reduce-scatter.2
  538.2 28.8 reduce-scatter.4
Sparse Core Ops, SparseCore 1:
  529.5 145.2 all-reduce.1
